TPU v7x, 512 devices: a whole 4x8x8 slice. The times are simulated.
512 devices in a mesh: row: 16 (over x, y_lo), col: 16 (over z, core), dp: 2 (over y_hi).
Axes of the slice: x: 4, y: 8 (y_hi: 2, y_lo: 4; y = y_hi * 4 + y_lo), z: 8, core: 2. Of those that a mesh axis runs over, the one named last changes fastest.
Arguments:
- grad_output: bfloat16 [2, 2048, 8192], P('dp', 'col', 'row'), may hold values from -0.09375 to 0.09375
- block_input: bfloat16 [2, 2048, 8192], P('dp', 'col', 'row'), may hold values from -6 to 6
- query_branch: bfloat16 [2, 2048, 8192], P('dp', 'row', 'col'), may hold values from -6 to 6
- key_branch: bfloat16 [2, 2048, 8192], P('dp', 'row', 'col'), may hold values from -6 to 6
- value_branch: bfloat16 [2, 2048, 8192], P('dp', 'row', 'col'), may hold values from -6 to 6
- out_weight: bfloat16 [8192, 8192], P('row', 'col'), may hold values from -0.0625 to 0.0625
- filters: float32 [512, 128], P('col'), may hold values from -0.5 to 0.5
Outputs:
- out_weight_grad: float32 [8192, 8192], P('row', 'col')
- value_weight_grad: float32 [8192, 8192], P('col', 'row')
- filter_grad: float32 [512, 128], P('col')
All inputs are finite; a program needn't handle non-finite values.
Results may differ from a plain program's by a relative error of at most 0.0029.
Values may be sent and summed in bfloat16 or wider, within the bound.
A program may use at most 128 MiB of HBM per device.

v0:
```python
import jax
import jax.numpy as jnp
from jax import lax
from jax.sharding import PartitionSpec as P

highest = lax.Precision.HIGHEST


def toeplitz(taps, tok_rows, causal):
    filter_len = taps.shape[1]
    out_pos = lax.broadcasted_iota(jnp.int32, (tok_rows, tok_rows + filter_len), 0)
    in_pos = lax.broadcasted_iota(jnp.int32, (tok_rows, tok_rows + filter_len), 1)
    lagged = out_pos + filter_len - in_pos if causal else in_pos - out_pos
    inside = (lagged >= 0) & (lagged < filter_len)
    picked = jnp.take(taps, jnp.clip(lagged, 0, filter_len - 1), axis=1)
    return jnp.where(inside[None], picked, 0.0)


def grouped_apply(table, signal, groups):
    blocks, extent, channels = signal.shape
    split = signal.reshape(blocks, extent, groups, channels // groups)
    result = jnp.einsum("gts,bsgc->btgc", table, split, precision=highest)
    return result.reshape(blocks, table.shape[1], channels)


def taps_partial(delta_mix, mixed_ext, groups, filter_len):
    blocks, tok_rows, channels = delta_mix.shape
    left_side = delta_mix.reshape(blocks, tok_rows, groups, channels // groups)
    right_side = mixed_ext.reshape(blocks, tok_rows + filter_len, groups, channels // groups)
    products = jnp.einsum("btgc,bsgc->gts", left_side, right_side, precision=highest)
    extent = tok_rows + filter_len
    flipped = products[:, :, ::-1]
    padded = jnp.pad(flipped, ((0, 0), (0, 0), (0, tok_rows)))
    flat_rows = padded.reshape(groups, -1)[:, : tok_rows * (extent + tok_rows - 1)]
    skewed = flat_rows.reshape(groups, tok_rows, extent + tok_rows - 1)
    column_sums = jnp.sum(skewed, axis=1)
    return column_sums[:, tok_rows - 1 : tok_rows - 1 + filter_len]


def local(grad_output, block_input, query_branch, key_branch, value_branch, out_weight, filters):
    filter_len = filters.shape[1]
    groups = filters.shape[0]
    tok_rows = query_branch.shape[1]
    channels = query_branch.shape[2]
    grads_all, inputs_all = (
        lax.all_gather(grad_output[0], "col", axis=0, tiled=True),
        lax.all_gather(block_input[0], "col", axis=0, tiled=True),
    )
    row_devices = lax.axis_size("row")
    sub_width = channels // row_devices
    delta_turned = lax.psum_scatter(
        lax.dot_general(
            out_weight, grads_all, (((0,), (1,)), ((), ())), preferred_element_type=jnp.float32
        ),
        "row",
        scatter_dimension=0,
        tiled=True,
    )
    queries, keys_here, values_here = (
        lax.all_to_all(query_branch[0], "row", split_axis=1, concat_axis=0, tiled=True),
        lax.all_to_all(key_branch[0], "row", split_axis=1, concat_axis=0, tiled=True),
        lax.all_to_all(value_branch[0], "row", split_axis=1, concat_axis=0, tiled=True),
    )
    delta_out = delta_turned.T
    local_groups = sub_width // (channels // groups)
    first_group = lax.axis_index("row") * local_groups
    my_taps = lax.dynamic_slice_in_dim(filters, first_group, local_groups, 0)
    mixed = keys_here.astype(jnp.float32) * values_here.astype(jnp.float32)
    mixed_blocks = mixed.reshape(row_devices, tok_rows, sub_width)
    earlier = jnp.concatenate(
        [
            jnp.zeros((1, filter_len, sub_width), jnp.float32),
            mixed_blocks[:-1, tok_rows - filter_len :],
        ],
        axis=0,
    )
    mixed_ext = jnp.concatenate([earlier, mixed_blocks], axis=1)
    conv_out = grouped_apply(toeplitz(my_taps, tok_rows, True), mixed_ext, local_groups).reshape(
        -1, sub_width
    )
    gated = (queries.astype(jnp.float32) * conv_out).astype(jnp.bfloat16)
    delta_mix = delta_out * queries.astype(jnp.float32)
    delta_blocks = delta_mix.reshape(row_devices, tok_rows, sub_width)
    later_part = jnp.concatenate(
        [delta_blocks[1:, :filter_len], jnp.zeros((1, filter_len, sub_width), jnp.float32)], axis=0
    )
    delta_ext = jnp.concatenate([delta_blocks, later_part], axis=1)
    delta_conv = grouped_apply(toeplitz(my_taps, tok_rows, False), delta_ext, local_groups).reshape(
        -1, sub_width
    )
    delta_value = (delta_conv * keys_here.astype(jnp.float32)).astype(jnp.bfloat16)
    my_terms = taps_partial(delta_blocks, mixed_ext, local_groups, filter_len)
    taps_local = lax.dynamic_update_slice_in_dim(
        jnp.zeros(filters.shape, jnp.float32), my_terms, first_group, 0
    )
    gated_all, value_all = (
        lax.all_gather(gated, "row", axis=1, tiled=True),
        lax.all_gather(delta_value, "row", axis=1, tiled=True),
    )
    out_grad = lax.dot_general(
        grads_all, gated_all, (((0,), (0,)), ((), ())), preferred_element_type=jnp.float32
    )
    value_grad = lax.dot_general(
        value_all, inputs_all, (((0,), (0,)), ((), ())), preferred_element_type=jnp.float32
    )
    out_grad, value_grad = lax.psum((out_grad, value_grad), "dp")
    taps_total = lax.psum(taps_local, ("row", "dp"))
    return (out_grad, value_grad, taps_total)


def solution(mesh):
    in_specs = (
        P("dp", "col", "row"),
        P("dp", "col", "row"),
        P("dp", "row", "col"),
        P("dp", "row", "col"),
        P("dp", "row", "col"),
        P("row", "col"),
        P("col", None),
    )
    out_specs = (P("row", "col"), P("col", "row"), P("col", None))
    return jax.shard_map(local, mesh=mesh, in_specs=in_specs, out_specs=out_specs, check_vma=False)
```

profile of v0, /device:TPU:64, one launch (start us, length us, event | category | flops | bytes accessed | tf_op | source)
XLA Modules:
  0.0 689.4 jit_solution(379694975442089937)
XLA Ops:
  8.0 48.5 %all-gather.11.cloned.1.call-done = bf16[1,2048,512]{2,1,0:T(8,128)(2,1)} async-done(((bf16[1,128,512]{2,1,0:T(8,128)(2,1)}), bf16[1,2048,512]{2,1,0:T(8,128)(2,1)}) %all-gather.11.cloned.1.call-update) | async-done | bytes 2097168 | tf_op jit(solution)/shard_map/all_gather | solution.py:46
  56.5 4.8 fusion.2
  61.4 0.9 copy-done.2
  62.2 0.8 copy.40
  63.0 7.1 %all-to-all-start.2 = ((bf16[128,16,32]{0,2,1:T(8,128)(2,1)}), bf16[128,16,32]{0,2,1:T(8,128)(2,1)S(1)}, u32[]{:S(2)}, u32[]{:S(2)}) async-start(bf16[128,16,32]{0,2,1:T(8,128)(2,1)} %bitcast.4), calls=%async_computation.2 | async-start | bytes 262144 | tf_op jit(solution)/shard_map/all_to_all | solution.py:62
  71.1 0.8 copy.38
  71.9 109.0 %gather_fusion = f32[32768,2]{1,0:T(8,128)} fusion(f32[2,128]{0,1:T(8,128)S(1)} %copy.62, s32[32768]{0:T(1024)S(1)} %broadcast_clamp_fusion.1), kind=kCustom, calls=%fused_computation.clone | custom fusion | bytes 655360 | tf_op jit(solution)/shard_map/jit(_take)/gather | solution.py:15
  180.9 10.0 %copy.46 = f32[128,256,2]{1,0,2:T(8,128)S(1)} copy(f32[128,256,2]{2,1,0:T(8,128)} %bitcast.113) | data formatting | bytes 524288 | tf_op jit(solution)/shard_map/jit(_take)/gather | solution.py:15
  190.9 0.8 copy.36
  191.9 7.5 %all-to-all-start.1 = ((bf16[128,16,32]{0,2,1:T(8,128)(2,1)}), bf16[128,16,32]{0,2,1:T(8,128)(2,1)S(1)}, u32[]{:S(2)}, u32[]{:S(2)}) async-start(bf16[128,16,32]{0,2,1:T(8,128)(2,1)} %bitcast.2), calls=%async_computation.1 | async-start | bytes 262144 | tf_op jit(solution)/shard_map/all_to_all | solution.py:61
  199.4 8.4 %all-to-all-done.1 = bf16[128,16,32]{0,2,1:T(8,128)(2,1)S(1)} async-done(((bf16[128,16,32]{0,2,1:T(8,128)(2,1)}), bf16[128,16,32]{0,2,1:T(8,128)(2,1)S(1)}, u32[]{:S(2)}, u32[]{:S(2)}) %all-to-all-start.1) | async-done | bytes 131104 | tf_op jit(solution)/shard_map/all_to_all | solution.py:61
  207.8 3.5 all-to-all-start
  212.4 7.3 %all-to-all-done = bf16[128,16,32]{0,2,1:T(8,128)(2,1)S(1)} async-done(((bf16[128,16,32]{0,2,1:T(8,128)(2,1)}), bf16[128,16,32]{0,2,1:T(8,128)(2,1)S(1)}, u32[]{:S(2)}, u32[]{:S(2)}) %all-to-all-start) | async-done | bytes 131104 | tf_op jit(solution)/shard_map/all_to_all | solution.py:60
  219.6 1.7 bitcast_multiply_fusion.2
  222.2 109.0 %gather_fusion.1 = f32[32768,2]{1,0:T(8,128)} fusion(f32[2,128]{0,1:T(8,128)S(1)} %copy.62, s32[32768]{0:T(1024)S(1)} %broadcast_clamp_fusion), kind=kCustom, calls=%fused_computation.1.clone | custom fusion | bytes 655360 | tf_op jit(solution)/shard_map/jit(_take)/gather | solution.py:15
  331.2 10.1 %copy.51 = f32[128,256,2]{1,0,2:T(8,128)S(1)} copy(f32[128,256,2]{2,1,0:T(8,128)} %bitcast.112) | data formatting | bytes 524288 | tf_op jit(solution)/shard_map/jit(_take)/gather | solution.py:15
  343.2 4.5 fusion.6
  347.7 1.5 all-gather.13.cloned.1.call-done
  349.2 91.4 %all-gather.9.cloned.1.call-done = bf16[2048,512]{0,1:T(8,128)(2,1)} async-done(((bf16[2048,32]{0,1:T(8,128)(2,1)}), bf16[2048,512]{0,1:T(8,128)(2,1)}) %all-gather.9.cloned.1.call-update) | async-done | bytes 2097168 | tf_op jit(solution)/shard_map/all_gather | solution.py:98
  440.6 4.4 fusion
  445.1 0.8 convolution_bitcast_fusion
  447.4 231.5 %psum.23 = f32[32,128]{1,0:T(8,128)} all-reduce(f32[32,128]{1,0:T(8,128)S(1)} %slice_dynamic-update-slice_fusion), channel_id=1, replica_groups=mesh['row'=16,'col'=16,'dp'=2] {'row','dp'}, use_global_device_ids=true, to_apply=%region_4.6 | all-reduce | flops 4096 | bytes 32768 | tf_op jit(solution)/shard_map/psum | solution.py:107
  678.9 2.6 copy.54
  681.5 1.0 copy.88
  (63 shorter events, 7.1 us)
Async XLA Ops:
  7.2 49.3 %copy-start = (bf16[512,512]{1,0:T(8,128)(2,1)S(1)}, bf16[512,512]{1,0:T(8,128)(2,1)}, u32[]{:S(2)}) copy-start(bf16[512,512]{1,0:T(8,128)(2,1)} %param.14) | copy-start | bytes 1572868
  7.2 49.3 %all-gather.11.cloned.1.call-start = ((), (), s32[]{:S(2)}) async-start(), calls=%async_computation.7 | async-start | bytes 2228224 | tf_op jit(solution)/shard_map/all_gather | solution.py:46
  7.9 211.7 %reduce-scatter.2.cloned.1.call-start = ((), (), s32[]{:S(2)}) async-start(), calls=%async_computation.5 | async-start | bytes 4456448 | tf_op jit(solution)/shard_map/reduce_scatter | solution.py:51
  61.3 0.9 copy-start.2
  61.3 9.7 %copy-start.3 = (bf16[1,128,512]{2,1,0:T(8,128)(2,1)S(1)}, bf16[1,128,512]{2,1,0:T(8,128)(2,1)}, u32[]{:S(2)}) copy-start(bf16[1,128,512]{2,1,0:T(8,128)(2,1)} %param.12) | copy-start | bytes 393220
  63.0 128.9 %all-to-all-start.2 = ((bf16[128,16,32]{0,2,1:T(8,128)(2,1)}), bf16[128,16,32]{0,2,1:T(8,128)(2,1)S(1)}, u32[]{:S(2)}, u32[]{:S(2)}) async-start(bf16[128,16,32]{0,2,1:T(8,128)(2,1)} %bitcast.4), calls=%async_computation.2 | async-start | bytes 262144 | tf_op jit(solution)/shard_map/all_to_all | solution.py:62
  180.9 10.0 %copy-start.4 = (bf16[1,128,512]{2,1,0:T(8,128)(2,1)S(1)}, bf16[1,128,512]{2,1,0:T(8,128)(2,1)}, u32[]{:S(2)}) copy-start(bf16[1,128,512]{2,1,0:T(8,128)(2,1)} %param.11) | copy-start | bytes 393220
  191.9 15.9 %all-to-all-start.1 = ((bf16[128,16,32]{0,2,1:T(8,128)(2,1)}), bf16[128,16,32]{0,2,1:T(8,128)(2,1)S(1)}, u32[]{:S(2)}, u32[]{:S(2)}) async-start(bf16[128,16,32]{0,2,1:T(8,128)(2,1)} %bitcast.2), calls=%async_computation.1 | async-start | bytes 262144 | tf_op jit(solution)/shard_map/all_to_all | solution.py:61
  207.8 11.9 %all-to-all-start = ((bf16[128,16,32]{0,2,1:T(8,128)(2,1)}), bf16[128,16,32]{0,2,1:T(8,128)(2,1)S(1)}, u32[]{:S(2)}, u32[]{:S(2)}) async-start(bf16[128,16,32]{0,2,1:T(8,128)(2,1)} %bitcast), calls=%async_computation | async-start | bytes 262144 | tf_op jit(solution)/shard_map/all_to_all | solution.py:60
  211.3 131.9 %all-gather.7.cloned.1.call-start = ((), (), s32[]{:S(2)}) async-start(), calls=%async_computation.4 | async-start | bytes 2228224 | tf_op jit(solution)/shard_map/all_gather | solution.py:97
  221.4 127.9 %all-gather.13.cloned.1.call-start = ((), (), s32[]{:S(2)}) async-start(), calls=%async_computation.8 | async-start | bytes 2228224 | tf_op jit(solution)/shard_map/all_gather | solution.py:47
  222.0 218.7 %all-gather.9.cloned.1.call-start = ((), (), s32[]{:S(2)}) async-start(), calls=%async_computation.6 | async-start | bytes 2228224 | tf_op jit(solution)/shard_map/all_gather | solution.py:98
  343.2 335.8 %all-reduce.6.cloned.1.call-start = ((), (), s32[]{:S(2)}) async-start(), calls=%async_computation.9 | async-start | bytes 4194304 | tf_op jit(solution)/shard_map/psum | solution.py:106
  678.9 2.6 copy-start.1
Sparse Core Ops, SparseCore 0:
  10.1 46.3 all-gather.10
  61.5 105.1 reduce-scatter.1
  221.5 84.2 all-gather.6
  307.8 41.4 all-gather.12
  351.7 88.8 all-gather.8
  445.2 122.4 all-reduce.5
where the time goes:
time: 690 us; the launch traced here: 689 us
  local copies, waits for them, and re-layouts  248 us (36%)
  blocking collectives  232 us (34%)
  waiting for transfers between devices  158 us (23%)
  starting transfers between devices  18.4 us (3%)
  matrix products  15.8 us (2%)
  between operations  14.4 us (2%)
    gather x4, local copies, waits for them, and re-layouts, toeplitz(): picked = jnp.take(taps, jnp.clip(lagged, 0, filter_len - 1), axis=1)  238 us
    psum x1, blocking collectives, local(): taps_total = lax.psum(taps_local, ('row', 'dp'))  232 us
    all_gather x1, waiting for transfers between devices, local(): lax.all_gather(delta_value, 'row', axis=1, tiled=True)  91.4 us
    all_gather x1, waiting for transfers between devices, local(): lax.all_gather(grad_output[0], 'col', axis=0, tiled=True)  48.5 us
  transfers between devices with their start and end apart: 9, of which 5 were waited for; matrix products, arithmetic and copies ran while one was open for 36% of the time, Pallas kernels for 0%

commit v1 on v0

--- a/solution.py
+++ b/solution.py
@@ -104,7 +104,7 @@
         value_all, inputs_all, (((0,), (0,)), ((), ())), preferred_element_type=jnp.float32
     )
     out_grad, value_grad = lax.psum((out_grad, value_grad), "dp")
-    taps_total = lax.psum(taps_local, ("row", "dp"))
+    taps_total = lax.psum(lax.psum(taps_local, "dp"), "row")
     return (out_grad, value_grad, taps_total)
 
 

time: 690 us -> 588 us (0.85)
  the two profiles are of different devices: /device:TPU:64 before, /device:TPU:1 now
where the time goes in v1:
time: 588 us; the launch traced here: 587 us
  local copies, waits for them, and re-layouts  246 us (42%)
  waiting for transfers between devices  203 us (35%)
  blocking collectives  87.1 us (15%)
  starting transfers between devices  17.5 us (3%)
  matrix products  15.8 us (3%)
  between operations  14.4 us (2%)
    gather x4, local copies, waits for them, and re-layouts, toeplitz(): picked = jnp.take(taps, jnp.clip(lagged, 0, filter_len - 1), axis=1)  237 us
    psum x2, blocking collectives, local(): taps_total = lax.psum(lax.psum(taps_local, 'dp'), 'row')  87.1 us
    all_gather x1, waiting for transfers between devices, local(): lax.all_gather(delta_value, 'row', axis=1, tiled=True)  81.3 us
    all_gather x1, waiting for transfers between devices, local(): lax.all_gather(grad_output[0], 'col', axis=0, tiled=True)  51.3 us
    psum x1, waiting for transfers between devices, local(): out_grad, value_grad = lax.psum((out_grad, value_grad), 'dp')  49.7 us
  transfers between devices with their start and end apart: 9, of which 6 were waited for; matrix products, arithmetic and copies ran while one was open for 43% of the time, Pallas kernels for 0%

profile of v1, /device:TPU:1, one launch (start us, length us, event | category | flops | bytes accessed | tf_op | source)
XLA Modules:
  0.0 587.0 jit_solution(16518102020407107777)
XLA Ops:
  8.0 51.3 %all-gather.11.cloned.1.call-done = bf16[1,2048,512]{2,1,0:T(8,128)(2,1)} async-done(((bf16[1,128,512]{2,1,0:T(8,128)(2,1)}), bf16[1,2048,512]{2,1,0:T(8,128)(2,1)}) %all-gather.11.cloned.1.call-update) | async-done | bytes 2097168 | tf_op jit(solution)/shard_map/all_gather | solution.py:46
  59.3 4.8 fusion.2
  64.1 0.9 copy-done.2
  65.8 6.8 %all-to-all-start.2 = ((bf16[128,16,32]{0,2,1:T(8,128)(2,1)}), bf16[128,16,32]{0,2,1:T(8,128)(2,1)S(1)}, u32[]{:S(2)}, u32[]{:S(2)}) async-start(bf16[128,16,32]{0,2,1:T(8,128)(2,1)} %bitcast.4), calls=%async_computation.2 | async-start | bytes 262144 | tf_op jit(solution)/shard_map/all_to_all | solution.py:62
  74.4 108.2 %gather_fusion = f32[32768,2]{1,0:T(8,128)} fusion(f32[2,128]{0,1:T(8,128)S(1)} %copy.62, s32[32768]{0:T(1024)S(1)} %broadcast_clamp_fusion.1), kind=kCustom, calls=%fused_computation.clone | custom fusion | bytes 655360 | tf_op jit(solution)/shard_map/jit(_take)/gather | solution.py:15
  182.7 10.0 %copy.46 = f32[128,256,2]{1,0,2:T(8,128)S(1)} copy(f32[128,256,2]{2,1,0:T(8,128)} %bitcast.113) | data formatting | bytes 524288 | tf_op jit(solution)/shard_map/jit(_take)/gather | solution.py:15
  192.6 0.8 copy.36
  193.6 7.0 %all-to-all-start.1 = ((bf16[128,16,32]{0,2,1:T(8,128)(2,1)}), bf16[128,16,32]{0,2,1:T(8,128)(2,1)S(1)}, u32[]{:S(2)}, u32[]{:S(2)}) async-start(bf16[128,16,32]{0,2,1:T(8,128)(2,1)} %bitcast.2), calls=%async_computation.1 | async-start | bytes 262144 | tf_op jit(solution)/shard_map/all_to_all | solution.py:61
  200.6 7.2 %all-to-all-done.1 = bf16[128,16,32]{0,2,1:T(8,128)(2,1)S(1)} async-done(((bf16[128,16,32]{0,2,1:T(8,128)(2,1)}), bf16[128,16,32]{0,2,1:T(8,128)(2,1)S(1)}, u32[]{:S(2)}, u32[]{:S(2)}) %all-to-all-start.1) | async-done | bytes 131104 | tf_op jit(solution)/shard_map/all_to_all | solution.py:61
  207.8 3.5 all-to-all-start
  212.4 6.1 %all-to-all-done = bf16[128,16,32]{0,2,1:T(8,128)(2,1)S(1)} async-done(((bf16[128,16,32]{0,2,1:T(8,128)(2,1)}), bf16[128,16,32]{0,2,1:T(8,128)(2,1)S(1)}, u32[]{:S(2)}, u32[]{:S(2)}) %all-to-all-start) | async-done | bytes 131104 | tf_op jit(solution)/shard_map/all_to_all | solution.py:60
  218.5 1.7 bitcast_multiply_fusion.2
  221.0 108.2 %gather_fusion.1 = f32[32768,2]{1,0:T(8,128)} fusion(f32[2,128]{0,1:T(8,128)S(1)} %copy.62, s32[32768]{0:T(1024)S(1)} %broadcast_clamp_fusion), kind=kCustom, calls=%fused_computation.1.clone | custom fusion | bytes 655360 | tf_op jit(solution)/shard_map/jit(_take)/gather | solution.py:15
  329.3 10.1 %copy.51 = f32[128,256,2]{1,0,2:T(8,128)S(1)} copy(f32[128,256,2]{2,1,0:T(8,128)} %bitcast.112) | data formatting | bytes 524288 | tf_op jit(solution)/shard_map/jit(_take)/gather | solution.py:15
  341.3 4.5 fusion.6
  345.8 5.9 all-gather.13.cloned.1.call-done
  351.7 81.3 %all-gather.9.cloned.1.call-done = bf16[2048,512]{0,1:T(8,128)(2,1)} async-done(((bf16[2048,32]{0,1:T(8,128)(2,1)}), bf16[2048,512]{0,1:T(8,128)(2,1)}) %all-gather.9.cloned.1.call-update) | async-done | bytes 2097168 | tf_op jit(solution)/shard_map/all_gather | solution.py:98
  432.9 4.4 fusion
  437.4 0.8 convolution_bitcast_fusion
  439.7 11.7 %psum.30 = f32[32,128]{1,0:T(8,128)S(1)} all-reduce(f32[32,128]{1,0:T(8,128)S(1)} %slice_dynamic-update-slice_fusion), channel_id=1, replica_groups=mesh['row'=16,'col'=16,'dp'=2] {'dp'}, use_global_device_ids=true, to_apply=%region_4.6 | all-reduce | flops 4096 | bytes 32768 | tf_op jit(solution)/shard_map/psum | solution.py:107
  451.4 75.4 %psum.31 = f32[32,128]{1,0:T(8,128)} all-reduce(f32[32,128]{1,0:T(8,128)S(1)} %psum.30), channel_id=1, replica_groups=mesh['row'=16,'col'=16,'dp'=2] {'row'}, use_global_device_ids=true, to_apply=%region_5.7 | all-reduce | flops 4096 | bytes 32768 | tf_op jit(solution)/shard_map/psum | solution.py:107
  526.8 49.7 %all-reduce.6.cloned.1.call-done = (f32[512,512]{0,1:T(8,128)}, f32[512,512]{1,0:T(8,128)}) async-done(((f32[512,512]{0,1:T(8,128)}, f32[512,512]{1,0:T(8,128)}), (f32[512,512]{0,1:T(8,128)}, f32[512,512]{1,0:T(8,128)})) %all-reduce.6.cloned.1.call-update) | async-done | bytes 2097168 | tf_op jit(solution)/shard_map/psum | solution.py:106
  576.5 2.6 copy.54
  579.2 1.0 copy.88
  (64 shorter events, 8.6 us)
Async XLA Ops:
  7.2 52.1 %copy-start = (bf16[512,512]{1,0:T(8,128)(2,1)S(1)}, bf16[512,512]{1,0:T(8,128)(2,1)}, u32[]{:S(2)}) copy-start(bf16[512,512]{1,0:T(8,128)(2,1)} %param.14) | copy-start | bytes 1572868
  7.2 52.1 %all-gather.11.cloned.1.call-start = ((), (), s32[]{:S(2)}) async-start(), calls=%async_computation.7 | async-start | bytes 2228224 | tf_op jit(solution)/shard_map/all_gather | solution.py:46
  7.9 210.6 %reduce-scatter.2.cloned.1.call-start = ((), (), s32[]{:S(2)}) async-start(), calls=%async_computation.5 | async-start | bytes 4456448 | tf_op jit(solution)/shard_map/reduce_scatter | solution.py:51
  64.1 0.9 copy-start.2
  64.1 9.4 %copy-start.3 = (bf16[1,128,512]{2,1,0:T(8,128)(2,1)S(1)}, bf16[1,128,512]{2,1,0:T(8,128)(2,1)}, u32[]{:S(2)}) copy-start(bf16[1,128,512]{2,1,0:T(8,128)(2,1)} %param.12) | copy-start | bytes 393220
  65.8 127.8 %all-to-all-start.2 = ((bf16[128,16,32]{0,2,1:T(8,128)(2,1)}), bf16[128,16,32]{0,2,1:T(8,128)(2,1)S(1)}, u32[]{:S(2)}, u32[]{:S(2)}) async-start(bf16[128,16,32]{0,2,1:T(8,128)(2,1)} %bitcast.4), calls=%async_computation.2 | async-start | bytes 262144 | tf_op jit(solution)/shard_map/all_to_all | solution.py:62
  182.6 10.0 %copy-start.4 = (bf16[1,128,512]{2,1,0:T(8,128)(2,1)S(1)}, bf16[1,128,512]{2,1,0:T(8,128)(2,1)}, u32[]{:S(2)}) copy-start(bf16[1,128,512]{2,1,0:T(8,128)(2,1)} %param.11) | copy-start | bytes 393220
  193.6 14.2 %all-to-all-start.1 = ((bf16[128,16,32]{0,2,1:T(8,128)(2,1)}), bf16[128,16,32]{0,2,1:T(8,128)(2,1)S(1)}, u32[]{:S(2)}, u32[]{:S(2)}) async-start(bf16[128,16,32]{0,2,1:T(8,128)(2,1)} %bitcast.2), calls=%async_computation.1 | async-start | bytes 262144 | tf_op jit(solution)/shard_map/all_to_all | solution.py:61
  207.8 10.7 %all-to-all-start = ((bf16[128,16,32]{0,2,1:T(8,128)(2,1)}), bf16[128,16,32]{0,2,1:T(8,128)(2,1)S(1)}, u32[]{:S(2)}, u32[]{:S(2)}) async-start(bf16[128,16,32]{0,2,1:T(8,128)(2,1)} %bitcast), calls=%async_computation | async-start | bytes 262144 | tf_op jit(solution)/shard_map/all_to_all | solution.py:60
  211.3 130.0 %all-gather.7.cloned.1.call-start = ((), (), s32[]{:S(2)}) async-start(), calls=%async_computation.4 | async-start | bytes 2228224 | tf_op jit(solution)/shard_map/all_gather | solution.py:97
  220.3 131.4 %all-gather.13.cloned.1.call-start = ((), (), s32[]{:S(2)}) async-start(), calls=%async_computation.8 | async-start | bytes 2228224 | tf_op jit(solution)/shard_map/all_gather | solution.py:47
  220.8 212.1 %all-gather.9.cloned.1.call-start = ((), (), s32[]{:S(2)}) async-start(), calls=%async_computation.6 | async-start | bytes 2228224 | tf_op jit(solution)/shard_map/all_gather | solution.py:98
  341.3 235.3 %all-reduce.6.cloned.1.call-start = ((), (), s32[]{:S(2)}) async-start(), calls=%async_computation.9 | async-start | bytes 4194304 | tf_op jit(solution)/shard_map/psum | solution.py:106
  576.5 2.6 copy-start.1
Sparse Core Ops, SparseCore 0:
  10.1 49.0 all-gather.10
  64.3 100.1 reduce-scatter.1
  220.4 77.4 all-gather.6
  299.9 51.7 all-gather.12
  354.2 78.7 all-gather.8
  437.5 138.9 all-reduce.5
